TPU v7x, 512 devices: a whole 4x8x8 slice. The times are simulated.
512 devices in a mesh: comp: 2 (over x_lo), tile: 128 (over z, x_hi, y), lev: 2 (over core).
Axes of the slice: x: 4 (x_hi: 2, x_lo: 2; x = x_hi * 2 + x_lo), y: 8, z: 8, core: 2. Of those that a mesh axis runs over, the one named last changes fastest.
Arguments:
- adj_final: float32 [2, 72, 32768], P('comp', 'lev', 'tile'), may hold values from -6 to 6
- flipped_vertical_steppers: float32 [2, 72, 72], P('comp', 'lev'), as said below
- profiles: float32 [2, 6, 72], P('comp', None, 'lev'), may hold values from -0.9 to 0.9
- skin_sensitivity_pair: float32 [2, 72], P('comp', 'lev'), may hold values from -0.9 to 0.9
- match: int32 [128], replicated, may hold values from 0 to 127, each once
- remap_offs: int32 [256, 4], P('tile'), may hold values from 0 to 5
- remap_count: int32 [256], P('tile'), may hold values from 1 to 4, as said below
- conserving_transfer_factors: float32 [256, 4, 128, 128], P('tile'), may hold values from -0.25 to 0.25
Outputs:
- adj_initial: float32 [2, 72, 32768], P('comp', 'lev', 'tile')
Inputs may be any that keep to these rules, and one draw needn't show every extreme that they name: `match`: the atmosphere tiles in some order, each once. `remap_offs`: entries at or past a row block's count are to be ignored. `remap_count`: some row block uses all 4 entries. `flipped_vertical_steppers`: off-diagonal entries weigh about as much as the diagonal in each row.
All inputs are finite; a program needn't handle non-finite values.
Results may differ from a plain program's by a relative error of at most 0.00014.
Values sent between devices are 32-bit elements; how exact they have to be, the bound alone decides.
A program may use at most 64 MiB of HBM per device.

v0:
```python
import jax
import jax.numpy as jnp
from jax import lax
from jax.sharding import PartitionSpec as P

STEPS = 6
NBMAX = 4


HIGH_ACCURACY = lax.Precision.HIGHEST


def passed_along(block, axis, distance):
    devices = range(lax.axis_size(axis))
    route = [(i - distance, i) for i in devices if i - distance in devices]
    return lax.ppermute(block, axis, route)


def hit_rows(target, count):
    spots = lax.broadcasted_iota(jnp.int32, (count, target.shape[0]), 0)
    return (spots == target[None, :]).astype(jnp.float32)


def level_adder(operator):

    def add_piece(total, piece, start):
        return jnp.dot(operator, piece, precision=HIGH_ACCURACY, preferred_element_type=jnp.float32)

    return add_piece


def on_device(
    adj_final,
    flipped_vertical_steppers,
    profiles,
    skin_sensitivity_pair,
    match,
    remap_offs,
    remap_count,
    conserving_transfer_factors,
):
    tile_blocks = remap_offs.shape[0]
    block = conserving_transfer_factors.shape[2]
    grid_cells = adj_final.shape[2]
    tiles = lax.axis_size("tile")
    blocks = tiles * tile_blocks
    entries = tile_blocks * NBMAX
    own_state = adj_final[0]
    operator = flipped_vertical_steppers[0]
    flux_rows = profiles[0]
    skin_factor_vector = skin_sensitivity_pair[0]
    add_levels = level_adder(operator)
    first_block = (match[lax.axis_index("tile")] - 1) * tile_blocks
    target = jnp.mod(first_block + remap_offs, blocks).reshape(entries)
    in_use = (
        lax.broadcasted_iota(jnp.int32, (tile_blocks, NBMAX), 1) < remap_count[:, None]
    ).astype(jnp.float32)
    partial_flux = jnp.dot(flux_rows, own_state, precision=HIGH_ACCURACY)
    phi_ocn = lax.psum(partial_flux, "lev")
    phi_rows = phi_ocn.reshape(STEPS, tile_blocks, block).transpose(1, 0, 2)
    contrib = (
        jnp.einsum("reij,rsi->resj", conserving_transfer_factors, phi_rows, precision=HIGH_ACCURACY)
        * in_use[:, :, None, None]
    )
    flat = contrib.reshape(entries, STEPS * block)
    mine = lax.psum_scatter(
        jnp.dot(
            hit_rows(target, tile_blocks * lax.axis_size("tile")), flat, precision=HIGH_ACCURACY
        ),
        "tile",
        scatter_dimension=0,
        tiled=True,
    )
    flux_atm = mine.reshape(tile_blocks, STEPS, block).transpose(1, 0, 2).reshape(STEPS, grid_cells)
    flux_atm = passed_along(flux_atm, "comp", -1)
    adjoint = own_state
    surface_part = jnp.zeros((grid_cells,), jnp.float32)
    for step in reversed(range(STEPS)):
        flux_now = flux_atm[step]
        adjoint = adjoint + flux_rows[step][:, None] * flux_now[None, :]
        surface_part = surface_part + jnp.dot(skin_factor_vector, adjoint, precision=HIGH_ACCURACY)
        adjoint = add_levels(
            jnp.zeros_like(adjoint),
            lax.all_gather(adjoint, "lev", axis=0, tiled=True),
            jnp.int32(0),
        )
    marine_share = add_levels(
        jnp.zeros_like(own_state),
        lax.all_gather(own_state, "lev", axis=0, tiled=True),
        jnp.int32(0),
    )
    surface_adj = lax.psum(surface_part, "lev")
    surface_adj = passed_along(surface_adj, "comp", 1)
    piece = lax.all_gather(surface_adj.reshape(tile_blocks, block), "tile", axis=0, tiled=True)
    hits = (
        target[:, None] == lax.broadcasted_iota(jnp.int32, (entries, piece.shape[0]), 1)
    ).astype(jnp.float32)
    chosen_tile_matrices = jnp.dot(hits, piece, precision=HIGH_ACCURACY)
    chosen_tile_matrices = (
        chosen_tile_matrices.reshape(tile_blocks, NBMAX, block) * in_use[:, :, None]
    )
    marine_skin_warmth = jnp.einsum(
        "dcfv,dcv->df", conserving_transfer_factors, chosen_tile_matrices, precision=HIGH_ACCURACY
    ).reshape(grid_cells)
    marine_tile_matrix = marine_share + skin_factor_vector[:, None] * marine_skin_warmth[None, :]
    is_atmos = lax.axis_index("comp") == 0
    return jnp.where(is_atmos, adjoint, marine_tile_matrix)[None]


def solution(mesh):
    return jax.shard_map(
        on_device,
        mesh=mesh,
        in_specs=(
            P("comp", "lev", "tile"),
            P("comp", "lev", None),
            P("comp", None, "lev"),
            P("comp", "lev"),
            P(),
            P("tile", None),
            P("tile"),
            P("tile", None, None, None),
        ),
        out_specs=P("comp", "lev", "tile"),
        check_vma=False,
    )
```

profile of v0, /device:TPU:2, one launch (start us, length us, event | category | flops | bytes accessed | tf_op | source)
XLA Modules:
  0.0 1725.5 jit_solution(2810413761851644490)
XLA Ops:
  6.5 0.7 copy-done.6
  7.3 0.6 dynamic_slice.3
  8.5 0.7 copy-done.5
  9.9 0.9 convolution_bitcast_fusion.6
  10.8 2.5 psum.14
  13.7 1.3 fusion.2
  15.0 1.3 dynamic-slice
  17.0 1322.4 %all-reduce.3.cloned.1.call-done = f32[256,768]{1,0:T(8,128)} async-done(((f32[256,768]{1,0:T(8,128)}), f32[256,768]{1,0:T(8,128)}) %all-reduce.3.cloned.1.call-update) | async-done | bytes 786448
  1339.4 0.7 constant_dynamic-slice_fusion
  1340.2 3.4 collective-permute-start
  1343.5 1.9 all-gather
  1345.5 1.9 all-gather.1
  1347.3 0.7 copy-done.1
  1348.3 1.9 all-gather.2
  1350.4 1.9 all-gather.3
  1352.6 1.9 all-gather.4
  1354.7 0.6 copy-done.4
  1356.2 1.9 all-gather.5
  1358.8 2.5 psum.15
  1361.2 1.3 collective-permute-start.1
  1362.5 1.9 all-gather.6
  1364.6 2.1 collective-permute-done.1
  1366.7 350.3 %all-gather.7 = f32[128,2,128]{2,1,0:T(2,128)S(1)} all-gather(f32[1,2,128]{2,1,0:T(2,128)S(1)} %bitcast.160), channel_id=1, replica_groups=mesh['comp'=2,'tile'=128,'lev'=2] {'tile'}, dimensions={0}, use_global_device_ids=true | all-gather | bytes 132096 | tf_op jit(solution)/shard_map/all_gather | solution.py:94
  1718.0 0.7 copy.14
  (52 shorter events, 5.0 us)
Async XLA Ops:
  6.5 6.8 copy-start
  6.5 1332.9 %all-reduce.3.cloned.1.call-start = ((), (), s32[]{:S(2)}) async-start(), calls=%async_computation | async-start | bytes 1572864
  6.5 0.7 copy-start.6
  8.5 0.7 copy-start.5
  9.2 0.7 copy-start.3
  9.2 0.7 copy-start.7
  15.0 1328.5 %copy-start.2 = (f32[1,36,256]{2,0,1:T(1,128)S(1)}, f32[1,36,256]{2,0,1:T(1,128)}, u32[]{:S(2)}) copy-start(f32[1,36,256]{2,0,1:T(1,128)} %param.8) | copy-start | bytes 110596
  1340.2 5.2 collective-permute-start
  1347.3 0.7 copy-start.1
  1354.6 0.7 copy-start.4
  1361.2 5.5 collective-permute-start.1
Sparse Core Ops, SparseCore 0:
  15.2 1324.1 all-reduce.2
where the time goes:
time: 1730 us
  waiting for transfers between devices  1320 us (76%)
  blocking collectives  368 us (21%)
    unnamed x2, waiting for transfers between devices  1320 us
    all_gather x1, blocking collectives, on_device(): lax.all_gather(surface_adj.reshape(tile_blocks, block), 'tile', axis=0, t...  350 us
  transfers between devices with their start and end apart: 3, of which 2 were waited for; matrix products, arithmetic and copies ran while one was open for 0% of the time, Pallas kernels for 0%

commit v1 on v0

v1 whole, which is shorter than its diff:
```python
import functools

import jax
import jax.numpy as jnp
from jax import lax
from jax.experimental import pallas as pl
from jax.experimental.pallas import tpu as pltpu
from jax.sharding import PartitionSpec as P

STEPS = 6
NBMAX = 4
HALF = STEPS // 2
F32 = jnp.float32
HIGHEST = lax.Precision.HIGHEST
MESH = pl.DeviceIdType.MESH


def dot(a, b):
    return jnp.dot(a, b, precision=HIGHEST, preferred_element_type=F32)


def column_of(row):
    n = row.shape[1]
    diagonal = lax.broadcasted_iota(jnp.int32, (n, n), 0) == lax.broadcasted_iota(
        jnp.int32, (n, n), 1
    )
    return jnp.sum(jnp.where(diagonal, row, 0.0), axis=1, keepdims=True)


def kernel(
    nz,
    nw,
    match_ref,
    offs_ref,
    count_ref,
    adj_ref,
    operator_ref,
    profile_ref,
    skin_ref,
    factors_hbm,
    out_ref,
    factors,
    state,
    operators,
    profiles,
    skins,
    flux_part,
    flux_half,
    contrib_in,
    row_out,
    row_in,
    sigma_own,
    sigma_row,
    pick_out,
    pick_in,
    powers,
    local_sem,
    pair_send,
    pair_recv,
    flux_send,
    flux_recv,
    contrib_send,
    contrib_recv,
    row_send,
    row_recv,
    sigma_send,
    sigma_recv,
    pick_send,
    pick_recv,
):
    comp = lax.axis_index("comp")
    lev = lax.axis_index("lev")
    tile = lax.axis_index("tile")
    tiles = nz * nw
    z = tile // nw
    w = tile % nw
    levels = adj_ref.shape[1]
    blk = factors.shape[2]
    rows = factors.shape[0]

    def remote(src, dst, send, recv, to_comp, to_tile, to_lev):
        copy = pltpu.make_async_remote_copy(
            src_ref=src,
            dst_ref=dst,
            send_sem=send,
            recv_sem=recv,
            device_id=(to_comp, to_tile, to_lev),
            device_id_type=MESH,
        )
        copy.start()

    def settle(ref, sem):
        pltpu.make_async_copy(ref, ref, sem).wait()

    load = pltpu.make_async_copy(factors_hbm, factors, local_sem)
    load.start()

    own = adj_ref[0]
    state[lev] = own

    @pl.when(comp == 1)
    def _():
        partial = dot(profile_ref[0], own)
        flux_part[0] = partial[:HALF]
        flux_part[1] = partial[HALF:]
        remote(flux_part.at[1 - lev], flux_half.at[lev], flux_send, flux_recv, 1, tile, 1 - lev)
        for half in range(2):
            remote(flux_part.at[half], flux_half.at[lev], flux_send, flux_recv, 0, tile, half)
        flux_half[lev] = flux_part[lev]

    operators[lev] = operator_ref[0]
    profiles[lev] = profile_ref[0]
    skins[lev] = skin_ref[...]
    for ref, i in ((state, 0), (operators, 1), (profiles, 2), (skins, 3)):
        remote(ref.at[lev], ref.at[lev], pair_send.at[i], pair_recv.at[i], comp, tile, 1 - lev)

    load.wait()

    @pl.when(comp == 1)
    def _():
        settle(flux_half.at[0], flux_recv)

    @pl.when(comp == 0)
    def _():
        settle(flux_half, flux_recv)

    flux = flux_half[0] + flux_half[1]
    flux = jnp.concatenate([flux, jnp.zeros((8 - HALF, flux.shape[1]), F32)], axis=0).T
    totals = [jnp.zeros((HALF, blk), F32) for _ in range(3)]
    for r in range(rows):
        columns = [
            jnp.broadcast_to(flux[r * blk : (r + 1) * blk, s : s + 1], (blk, blk))
            for s in range(HALF)
        ]
        for e in range(NBMAX):
            block = factors[r, e]
            part = jnp.concatenate(
                [jnp.sum(block * columns[s], axis=0, keepdims=True) for s in range(HALF)], axis=0
            )
            offset = offs_ref[r, e]
            used = e < count_ref[r]
            for d in range(3):
                take = jnp.logical_and(used, offset == 2 * d + comp)
                totals[d] = totals[d] + part * take.astype(F32)
    for d in range(3):
        contrib_in[z, d] = totals[d]
    for k in range(1, nz):
        to = (z + k) % nz
        remote(
            contrib_in.at[z], contrib_in.at[z], contrib_send, contrib_recv, comp, to * nw + w, lev
        )

    held = [match_ref[i * nw + w] for i in range(nz)]
    origin, present = [], []
    for p in range(nw + 2):
        wanted = (z * nw - 1 + p + tiles) % tiles
        found = jnp.int32(-1)
        for i in range(nz):
            found = jnp.where(held[i] == wanted, i, found)
        origin.append(jnp.maximum(found, 0))
        present.append((found >= 0).astype(F32))

    for i, ref in enumerate((state, operators, profiles, skins)):
        settle(ref.at[0], pair_recv.at[i])
    whole = jnp.concatenate([operators[0], operators[1]], axis=0)
    skin_row = jnp.concatenate([skins[0], skins[1]], axis=1)
    profile_rows = jnp.concatenate([profiles[0], profiles[1]], axis=1)
    powers[0, :levels] = operator_ref[0]
    powers[0, levels : levels + 1] = skin_row

    @pl.when(comp == 0)
    def _():
        held_power = powers[0, : levels + 1]
        last = held_power[levels:]
        for n in range(1, STEPS):
            held_power = dot(held_power, whole)
            last = last + held_power[levels:]
            powers[n, :levels] = held_power[:levels]
            powers[n, levels : levels + 1] = last

    settle(contrib_in.at[: nz - 1], contrib_recv)

    for q in range(nw):
        total = jnp.zeros((HALF, blk), F32)
        for d in range(3):
            p = q + 2 - d
            total = total + contrib_in[origin[p], d] * present[p]
        row_out[q] = total
    slot = (comp * 2 + lev) * nw + w
    for k in range(nw):
        to = (w + k) % nw
        for half in range(2):
            if k == 0:
                here = jnp.logical_and(comp == 0, lev == half)

                @pl.when(here)
                def _():
                    row_in[slot] = row_out[w]

                @pl.when(jnp.logical_not(here))
                def _():
                    remote(
                        row_out.at[to], row_in.at[slot], row_send, row_recv, 0, z * nw + to, half
                    )

            else:
                remote(row_out.at[to], row_in.at[slot], row_send, row_recv, 0, z * nw + to, half)

    full_state = jnp.concatenate([state[0], state[1]], axis=0)

    @pl.when(comp == 0)
    def _():
        base = dot(powers[STEPS - 1, : levels + 1], full_state)
        shares = [
            jnp.sum(powers[s, : levels + 1] * profile_rows[s : s + 1], axis=1, keepdims=True)
            for s in range(STEPS)
        ]
        settle(row_in.at[: 4 * nw - 1], row_recv)
        halves = []
        for parity in range(2):
            cells = slice(parity * blk, (parity + 1) * blk)
            total = base[:, cells]
            for half in range(2):
                start = (parity * 2 + half) * nw
                flux_sum = row_in[start]
                for k in range(1, nw):
                    flux_sum = flux_sum + row_in[start + k]
                for s in range(HALF):
                    total = total + shares[half * HALF + s] * flux_sum[s : s + 1]
            sigma_own[parity : parity + 1] = total[levels:]
            halves.append(total)
        for k in range(nw):
            to = (w + k) % nw
            remote(sigma_own, sigma_row.at[w], sigma_send, sigma_recv, 1, z * nw + to, lev)
        for parity in range(2):
            out_ref[0, :, parity * blk : (parity + 1) * blk] = halves[parity][:levels]

    @pl.when(comp == 1)
    def _():
        base = dot(powers[0, :levels], full_state)
        settle(sigma_row, sigma_recv)
        for i in range(nz):
            first = match_ref[i * nw + w] - 1 + tiles
            for d in range(3):
                pick_out[i, d] = sigma_row[(first + d) % nw]
        for k in range(1, nz):
            to = (z + k) % nz
            remote(pick_out.at[to], pick_in.at[z], pick_send, pick_recv, 1, to * nw + w, lev)
        pick_in[z] = pick_out[z]
        settle(pick_in.at[: nz - 1], pick_recv)
        first = match_ref[tile] - 1 + tiles
        home = [((first + d) % tiles) // nw for d in range(3)]
        skin_column = jnp.broadcast_to(column_of(skin_ref[...]), (levels, blk))
        for r in range(rows):
            total = jnp.zeros((blk, blk), F32)
            for e in range(NBMAX):
                offset = offs_ref[r, e]
                used = (e < count_ref[r]).astype(F32)
                third = offset // 2
                where = jnp.where(third == 0, home[0], jnp.where(third == 1, home[1], home[2]))
                sigma = pick_in[where, third, pl.ds(offset % 2, 1)] * used
                total = total + factors[r, e] * sigma
            warmth = lax.dot_general(
                skin_column,
                total,
                (((1,), (1,)), ((), ())),
                precision=HIGHEST,
                preferred_element_type=F32,
            )
            cells = slice(r * blk, (r + 1) * blk)
            out_ref[0, :, cells] = base[:, cells] + warmth

    for i, ref in enumerate((state, operators, profiles, skins)):
        settle(ref.at[0], pair_send.at[i])
    settle(contrib_in.at[: nz - 1], contrib_send)

    @pl.when(comp == 0)
    def _():
        settle(row_in.at[: 2 * nw - 1], row_send)
        settle(sigma_row, sigma_send)

    @pl.when(comp == 1)
    def _():
        settle(row_in.at[: 2 * nw], row_send)
        settle(flux_part, flux_send)
        settle(pick_in.at[: nz - 1], pick_send)


def on_device(
    adj_final,
    flipped_vertical_steppers,
    profiles,
    skin_sensitivity_pair,
    match,
    remap_offs,
    remap_count,
    conserving_transfer_factors,
):
    tiles = lax.axis_size("tile")
    nz = 2 ** ((tiles.bit_length() - 1) // 2)
    nw = tiles // nz
    levels, cells = adj_final.shape[1:]
    rows, _, blk, _ = conserving_transfer_factors.shape
    vmem = pl.BlockSpec(memory_space=pltpu.VMEM)
    smem = pl.BlockSpec(memory_space=pltpu.SMEM)
    dma = pltpu.SemaphoreType.DMA
    return pl.pallas_call(
        functools.partial(kernel, nz, nw),
        out_shape=jax.ShapeDtypeStruct(adj_final.shape, F32),
        in_specs=[smem] * 3 + [vmem] * 4 + [pl.BlockSpec(memory_space=pl.ANY)],
        out_specs=vmem,
        scratch_shapes=[
            pltpu.VMEM((rows, NBMAX, blk, blk), F32),
            pltpu.VMEM((2, levels, cells), F32),
            pltpu.VMEM((2, levels, 2 * levels), F32),
            pltpu.VMEM((2, STEPS, levels), F32),
            pltpu.VMEM((2, 1, levels), F32),
            pltpu.VMEM((3, HALF, cells), F32),
            pltpu.VMEM((2, HALF, cells), F32),
            pltpu.VMEM((nz, 3, HALF, blk), F32),
            pltpu.VMEM((nw, HALF, blk), F32),
            pltpu.VMEM((4 * nw, HALF, blk), F32),
            pltpu.VMEM((2, blk), F32),
            pltpu.VMEM((nw, 2, blk), F32),
            pltpu.VMEM((nz, 3, 2, blk), F32),
            pltpu.VMEM((nz, 3, 2, blk), F32),
            pltpu.VMEM((STEPS, levels + 4, 2 * levels), F32),
            dma,
            dma((4,)),
            dma((4,)),
        ]
        + [dma] * 10,
        compiler_params=pltpu.CompilerParams(has_side_effects=True, vmem_limit_bytes=32 << 20),
    )(
        match,
        remap_offs,
        remap_count,
        adj_final,
        flipped_vertical_steppers,
        profiles,
        skin_sensitivity_pair,
        conserving_transfer_factors,
    )


def solution(mesh):
    return jax.shard_map(
        on_device,
        mesh=mesh,
        in_specs=(
            P("comp", "lev", "tile"),
            P("comp", "lev", None),
            P("comp", None, "lev"),
            P("comp", "lev"),
            P(),
            P("tile", None),
            P("tile"),
            P("tile", None, None, None),
        ),
        out_specs=P("comp", "lev", "tile"),
        check_vma=False,
    )
```

time: 1730 us -> 52 us (0.03)
  waiting for transfers between devices: 1320 us -> 0 us
  blocking collectives: 368 us -> 0 us
  Pallas kernels: 0 us -> 47.8 us
    unnamed x2 -> x0, waiting for transfers between devices: 1320 us -> none
    all_gather x8 -> x0, blocking collectives: 363 us -> none  [the longest x1 350 us: on_device(): lax.all_gather(surface_adj.reshape(tile_blocks, block), 'tile', axis=0, t...]
    pallas_call x0 -> x1, Pallas kernels: none -> 47.8 us  [on_device(): pl.pallas_call(functools.partial(kernel, nz, nw), out_shape=jax.ShapeDtyp...]
  transfers between devices with their start and end apart: 3 -> 0, of which waited for: 2 -> 0; matrix products, arithmetic and copies ran while one was open for 0% -> 0% of each run, Pallas kernels for 0% -> 0%
where the time goes in v1:
time: 52 us; the launch traced here: 51.7 us
  Pallas kernels  47.8 us (92%)
  local copies, waits for them, and re-layouts  3.79 us (7%)
    pallas_call x1, Pallas kernels, on_device(): pl.pallas_call(functools.partial(kernel, nz, nw), out_shape=jax.ShapeDtyp...  47.8 us
    unnamed x15, local copies, waits for them, and re-layouts  3.13 us

profile of v1, /device:TPU:2, one launch (start us, length us, event | category | flops | bytes accessed | tf_op | source)
XLA Modules:
  0.0 51.7 jit_solution(13879474476285203103)
XLA Ops:
  0.0 0.0 copy-start.5
  0.0 0.7 %copy.11.profile_ref = f32[1,6,36]{2,1,0:T(8,128)S(1)} copy(f32[1,6,36]{2,0,1:T(1,128)} %param.10) | data formatting | bytes 1728 | tf_op args[2]
  0.7 0.7 %copy.10.operator_ref = f32[1,36,72]{2,1,0:T(8,128)S(1)} copy(f32[1,36,72]{2,0,1:T(1,128)} %param.9) | data formatting | bytes 20736 | tf_op args[1]
  1.4 0.0 copy-done.5
  1.4 0.0 copy-start.1
  1.4 0.0 copy-start.2
  1.4 0.0 copy-start.3
  1.4 0.0 copy-start.4
  1.5 0.6 %copy-done.1 = s32[2,4]{1,0:T(2,128)S(1)} copy-done((s32[2,4]{1,0:T(2,128)S(1)}, s32[2,4]{1,0:T(2,128)}, u32[]{:S(2)}) %copy-start.1) | copy-done | bytes 56
  2.1 0.0 copy-done.2
  2.1 0.0 copy-done.3
  2.1 0.0 copy-done.4
  2.1 0.0 copy-start
  2.1 1.0 %copy-done = f32[2,4,128,128]{3,2,1,0:T(8,128)S(1)} copy-done((f32[2,4,128,128]{3,2,1,0:T(8,128)S(1)}, f32[2,4,128,128]{3,2,1,0:T(8,128)}, u32[]{:S(2)}) %copy-start) | copy-done | bytes 524312
  3.2 47.8 %shard_map.82 = f32[1,36,256]{2,1,0:T(8,128)S(1)} custom-call(s32[128]{0:T(128)S(1)} %copy-done.2, s32[2,4]{1,0:T(2,128)S(1)} %copy-done.1, s32[2]{0:T(128)S(1)} %copy-done.3, f32[1,36,256]{2,1,0:T(8,128)S(1)} %copy.9.adj_ref, f32[1,36,72]{2,1,0:T(8,128)S(1)} %copy.10.operator_ref, f32[1,6,36]{2,1,0:T(8,128)S(1)} %copy.11.profile_ref, ...), custom_call_target="tpu_custom_call" | custom-call | tf_op jit(solution)/shard_map/pallas_call | solution.py:307
  51.0 0.7 %copy.12 = f32[1,36,256]{2,0,1:T(1,128)} copy(f32[1,36,256]{2,1,0:T(8,128)S(1)} %shard_map.82) | data formatting | bytes 73728 | tf_op jit(solution)/shard_map/pallas_call | solution.py:307
  (1 shorter events, 0.0 us)
Async XLA Ops:
  0.0 1.4 %copy-start.5 = (f32[1,36,256]{2,0,1:T(1,128)S(1)}, f32[1,36,256]{2,0,1:T(1,128)}, u32[]{:S(2)}) copy-start(f32[1,36,256]{2,0,1:T(1,128)} %param.8) | copy-start | bytes 110596
  1.4 0.7 %copy-start.1 = (s32[2,4]{1,0:T(2,128)S(1)}, s32[2,4]{1,0:T(2,128)}, u32[]{:S(2)}) copy-start(s32[2,4]{1,0:T(2,128)} %offs_ref.1) | copy-start | bytes 100
  1.4 0.7 %copy-start.2 = (s32[128]{0:T(128)S(1)}, s32[128]{0:T(128)}, u32[]{:S(2)}) copy-start(s32[128]{0:T(128)} %match_ref.1) | copy-start | bytes 1540
  1.4 0.7 %copy-start.3 = (s32[2]{0:T(128)S(1)}, s32[2]{0:T(128)}, u32[]{:S(2)}) copy-start(s32[2]{0:T(128)} %count_ref.1) | copy-start | bytes 28
  1.4 0.7 %copy-start.4 = (f32[1,36]{1,0:T(1,128)S(1)}, f32[1,36]{1,0:T(1,128)}, u32[]{:S(2)}) copy-start(f32[1,36]{1,0:T(1,128)} %skin_ref.1) | copy-start | bytes 436
  2.1 1.0 %copy-start = (f32[2,4,128,128]{3,2,1,0:T(8,128)S(1)}, f32[2,4,128,128]{3,2,1,0:T(8,128)}, u32[]{:S(2)}) copy-start(f32[2,4,128,128]{3,2,1,0:T(8,128)} %factors_hbm.1) | copy-start | bytes 1572868

commit v2 on v0

v2 whole, which is shorter than its diff:
```python
import functools

import jax
import jax.numpy as jnp
from jax import lax
from jax.experimental import pallas as pl
from jax.experimental.pallas import tpu as pltpu
from jax.sharding import PartitionSpec as P

STEPS = 6
NBMAX = 4
HALF = STEPS // 2
F32 = jnp.float32
HIGHEST = lax.Precision.HIGHEST
MESH = pl.DeviceIdType.MESH
REACH = 6
GROUP = 8


def dot(a, b):
    return jnp.dot(a, b, precision=HIGHEST, preferred_element_type=F32)


def column_of(row):
    n = row.shape[1]
    diagonal = lax.broadcasted_iota(jnp.int32, (n, n), 0) == lax.broadcasted_iota(
        jnp.int32, (n, n), 1
    )
    return jnp.sum(jnp.where(diagonal, row, 0.0), axis=1, keepdims=True)


def kernel(
    nz,
    nw,
    match_hbm,
    offs_hbm,
    count_hbm,
    adj_hbm,
    operator_hbm,
    profile_hbm,
    skin_hbm,
    factors_hbm,
    out_ref,
    match_ref,
    offs_ref,
    count_ref,
    factors,
    state,
    operators,
    profiles,
    skins,
    flux_part,
    flux_half,
    contrib_in,
    weight_in,
    sigma_own,
    sigma_in,
    mixed,
    flux_out,
    flux_in,
    flux_sum,
    heat_out,
    heat_in,
    heat_sum,
    heat,
    load_sem,
    pair_send,
    pair_recv,
    part_send,
    part_recv,
    contrib_send,
    contrib_recv,
    weight_send,
    weight_recv,
    sigma_send,
    sigma_recv,
    flux_send,
    flux_recv,
    heat_send,
    heat_recv,
    last_send,
    last_recv,
):
    comp = lax.axis_index("comp")
    lev = lax.axis_index("lev")
    tile = lax.axis_index("tile")
    tiles = nz * nw
    z = tile // nw
    w = tile % nw
    levels = operators.shape[1]
    blk = factors.shape[2]
    rows = factors.shape[0]
    column = [((z + k) % nz) * nw + w for k in range(nz)]
    row = [z * nw + (w + k) % nw for k in range(nw)]
    atmos, ocean = comp == 0, comp == 1

    def remote(src, dst, send, recv, to_comp, to_tile, to_lev):
        pltpu.make_async_remote_copy(
            src_ref=src,
            dst_ref=dst,
            send_sem=send,
            recv_sem=recv,
            device_id=(to_comp, to_tile, to_lev),
            device_id_type=MESH,
        ).start()

    def settle(ref, sem):
        pltpu.make_async_copy(ref, ref, sem).wait()

    def halves(ref):
        return [ref[pl.ds(h, levels, stride=2), :] for h in range(2)]

    loads = [
        pltpu.make_async_copy(src, dst, load_sem.at[i])
        for i, (src, dst) in enumerate(
            (
                (adj_hbm, state.at[lev]),
                (profile_hbm.at[0], profiles.at[lev]),
                (operator_hbm.at[0], operators.at[lev]),
                (skin_hbm, skins.at[lev]),
                (factors_hbm, factors),
                (offs_hbm, offs_ref),
                (count_hbm, count_ref),
                (match_hbm, match_ref),
            )
        )
    ]
    for load in loads:
        load.start()

    barrier = pltpu.get_barrier_semaphore()

    def greet(to_comp, to_tile, to_lev):
        pl.semaphore_signal(
            barrier, inc=1, device_id=(to_comp, to_tile, to_lev), device_id_type=MESH
        )

    greet(comp, tile, 1 - lev)

    @pl.when(atmos)
    def _():
        for to in row:
            greet(1, to, lev)
        pl.semaphore_wait(barrier, 1 + nz)

    @pl.when(ocean)
    def _():
        for to in column:
            greet(0, to, lev)
        for to in column[1:] + row[1:]:
            greet(1, to, lev)
        pl.semaphore_wait(barrier, nz + 2 * nw - 1)

    pairs = (
        (adj_hbm, state),
        (operator_hbm.at[0], operators),
        (profile_hbm.at[0], profiles),
        (skin_hbm, skins),
    )

    @pl.when(atmos)
    def _():
        for i, (src, dst) in ((1, pairs[1]), (3, pairs[3]), (2, pairs[2]), (0, pairs[0])):
            remote(src, dst.at[lev], pair_send.at[i], pair_recv.at[i], 0, tile, 1 - lev)
        for load in loads[:4]:
            load.wait()
        for i in (1, 2, 3):
            settle(pairs[i][1].at[0], pair_recv.at[i])
        whole = jnp.concatenate([operators[0], operators[1]], axis=0)
        profile_rows = jnp.concatenate([profiles[0], profiles[1]], axis=1)

        power = jnp.concatenate([skins[0], skins[1]], axis=1)
        total = power
        for s in range(STEPS):
            if s > 0:
                power = dot(power, whole)
                total = total + power
            weight = jnp.sum(total * profile_rows[s : s + 1], axis=1, keepdims=True)
            weight_in[1, s : s + 1] = jnp.broadcast_to(weight, (1, blk))
        remote(weight_in.at[1], weight_in.at[0], weight_send, weight_recv, 1, tile, lev)
        mine = jnp.where(lev == 0, total[:, :levels], total[:, levels:])
        own = halves(state.at[lev])
        for h in range(2):
            sigma_own[h : h + 1] = dot(mine, own[h])
        for to in column:
            remote(sigma_own, sigma_in.at[z], sigma_send, sigma_recv, 1, to, lev)

        power = operators[lev]
        shares = []
        for s in range(STEPS):
            if s > 0:
                power = dot(power, whole)
            shares.append(jnp.sum(power * profile_rows[s : s + 1], axis=1, keepdims=True))
        settle(state.at[0], pair_recv.at[0])
        first, second = halves(state.at[0]), halves(state.at[1])
        bases = [dot(power, jnp.concatenate([first[h], second[h]], axis=0)) for h in range(2)]

        settle(flux_in, flux_recv)
        total = flux_in[0]
        for k in range(1, nw):
            total = total + flux_in[k]
        flux_sum[lev] = total
        remote(flux_sum.at[lev], flux_sum.at[lev], last_send, last_recv, 0, tile, 1 - lev)
        settle(flux_sum.at[0], last_recv)
        for h in range(2):
            total = bases[h]
            for s in range(STEPS):
                total = total + shares[s] * flux_sum[s // HALF, s % HALF, h : h + 1]
            out_ref[pl.ds(h, levels, stride=2), :] = total

        for i in range(4):
            settle(pairs[i][1].at[0], pair_send.at[i])
        settle(weight_in.at[0], weight_send)
        settle(sigma_in, sigma_send)
        settle(flux_sum.at[0], last_send)
        for load in loads[4:]:
            load.wait()

    @pl.when(ocean)
    def _():
        for load in loads[:2]:
            load.wait()
        own = halves(state.at[lev])
        for h in range(2):
            partial = dot(profiles[lev], own[h])
            for half in range(2):
                flux_part[half, h] = partial[half * HALF : (half + 1) * HALF]
        remote(
            flux_part.at[1 - lev], flux_half.at[lev], part_send, part_recv, 1, tile, 1 - lev
        )
        remote(adj_hbm, state.at[lev], pair_send.at[0], pair_recv.at[0], 1, tile, 1 - lev)
        flux_half[lev] = flux_part[lev]
        contrib_in[:, :, REACH:] = jnp.zeros((nz, HALF, GROUP - REACH, blk), F32)
        for load in loads[4:]:
            load.wait()
        settle(flux_half.at[0], part_recv)

        totals = [jnp.zeros((HALF, blk), F32) for _ in range(REACH)]
        for r in range(rows):
            flux = flux_half[0, r] + flux_half[1, r]
            flux = jnp.concatenate([flux, jnp.zeros((GROUP - HALF, blk), F32)], axis=0).T
            columns = [jnp.broadcast_to(flux[:, s : s + 1], (blk, blk)) for s in range(HALF)]
            for e in range(NBMAX):
                block = factors[r, e]
                part = jnp.concatenate(
                    [jnp.sum(block * columns[s], axis=0, keepdims=True) for s in range(HALF)],
                    axis=0,
                )
                offset = jnp.where(e < count_ref[r], offs_ref[r, e], -1)
                for b in range(REACH):
                    totals[b] = totals[b] + part * (offset == b).astype(F32)
        for s in range(HALF):
            contrib_in[z, s, :REACH] = jnp.concatenate(
                [totals[b][s : s + 1] for b in range(REACH)], axis=0
            )
        for to in column[1:]:
            remote(
                contrib_in.at[z, :, pl.ds(0, REACH)],
                contrib_in.at[z, :, pl.ds(0, REACH)],
                contrib_send,
                contrib_recv,
                1,
                to,
                lev,
            )

        size = nz * GROUP
        lane = lax.broadcasted_iota(jnp.int32, (GROUP, size), 1)
        sub = lax.broadcasted_iota(jnp.int32, (GROUP, size), 0)
        place, source = lane % GROUP, lane // GROUP
        have = jnp.zeros((GROUP, size), jnp.int32)
        for i in range(nz):
            have = jnp.where(source == i, match_ref[i * nw + w] - 1, have)
        have = jnp.where(place < REACH, have + place // 2, source * nw + w)
        same = (lane % 2) == (sub % 2)
        picks = []
        for q in range(0, nw, 4):
            wanted = z * nw + q + sub // 2
            hit = jnp.bitwise_and(have - wanted, tiles - 1) == 0
            hit = jnp.logical_and(jnp.logical_and(hit, same), place < REACH)
            picks.append(hit.astype(F32))
        to_atmos = jnp.concatenate(picks, axis=0)[: 2 * nw]
        picks = []
        for q in range(nw):
            wanted = match_ref[z * nw + q] - 1 + sub // 2
            hit = jnp.bitwise_and(have - wanted, tiles - 1) == 0
            hit = jnp.logical_and(jnp.logical_and(hit, same), sub < REACH)
            picks.append(hit.astype(F32))
        to_ocean = jnp.concatenate(picks, axis=0)

        for load in loads[2:4]:
            load.wait()
        settle(state.at[0], pair_recv.at[0])
        first, second = halves(state.at[0]), halves(state.at[1])
        bases = [
            dot(operators[lev], jnp.concatenate([first[h], second[h]], axis=0)) for h in range(2)
        ]
        skin_column = jnp.broadcast_to(column_of(skins[lev]), (levels, blk))

        settle(contrib_in.at[: nz - 1, :, pl.ds(0, REACH)], contrib_recv)
        column_data = [contrib_in[:, s].reshape(size, blk) for s in range(HALF)]
        for s in range(HALF):
            picked = dot(to_atmos, column_data[s])
            for q in range(nw):
                flux_out[q, s] = picked[2 * q : 2 * q + 2]
        for k in range(nw):
            remote(
                flux_out.at[(w + k) % nw], flux_in.at[w], flux_send, flux_recv, 0, row[k], lev
            )
        settle(weight_in.at[0], weight_recv)
        total = jnp.zeros((size, blk), F32)
        for s in range(HALF):
            weight = jnp.where(
                lev == 0, weight_in[0, s : s + 1], weight_in[0, HALF + s : HALF + s + 1]
            )
            total = total + weight * column_data[s]
        mixed[...] = total
        settle(sigma_in, sigma_recv)
        for i in range(nz):
            mixed[i * GROUP + REACH : (i + 1) * GROUP] = sigma_in[i]
        heat_out[...] = dot(to_ocean, mixed[...]).reshape(nw, GROUP, blk)
        for k in range(1, nw):
            remote(
                heat_out.at[(w + k) % nw], heat_in.at[w], heat_send, heat_recv, 1, row[k], lev
            )
        heat_in[w] = heat_out[w]
        settle(heat_in.at[: nw - 1], heat_recv)
        total = heat_in[0]
        for k in range(1, nw):
            total = total + heat_in[k]
        heat_sum[lev] = total
        remote(heat_sum.at[lev], heat_sum.at[lev], last_send, last_recv, 1, tile, 1 - lev)
        settle(heat_sum.at[0], last_recv)
        heat[...] = heat_sum[0] + heat_sum[1]
        for r in range(rows):
            total = jnp.zeros((blk, blk), F32)
            for e in range(NBMAX):
                used = (e < count_ref[r]).astype(F32)
                total = total + factors[r, e] * (heat[pl.ds(offs_ref[r, e], 1), :] * used)
            warmth = lax.dot_general(
                skin_column,
                total,
                (((1,), (1,)), ((), ())),
                precision=HIGHEST,
                preferred_element_type=F32,
            )
            out_ref[pl.ds(r, levels, stride=2), :] = bases[r] + warmth

        settle(flux_part.at[0], part_send)
        settle(state.at[0], pair_send.at[0])
        settle(contrib_in.at[: nz - 1, :, pl.ds(0, REACH)], contrib_send)
        settle(flux_in, flux_send)
        settle(heat_in.at[: nw - 1], heat_send)
        settle(heat_sum.at[0], last_send)


def on_device(
    adj_final,
    flipped_vertical_steppers,
    profiles,
    skin_sensitivity_pair,
    match,
    remap_offs,
    remap_count,
    conserving_transfer_factors,
):
    tiles = lax.axis_size("tile")
    nz = 2 ** ((tiles.bit_length() - 1) // 2)
    nw = tiles // nz
    levels, cells = adj_final.shape[1:]
    rows, _, blk, _ = conserving_transfer_factors.shape
    hbm = pl.BlockSpec(memory_space=pltpu.HBM)
    dma = pltpu.SemaphoreType.DMA
    out = pl.pallas_call(
        functools.partial(kernel, nz, nw),
        out_shape=jax.ShapeDtypeStruct((levels * rows, blk), F32),
        in_specs=[hbm] * 8,
        out_specs=pl.BlockSpec(memory_space=pltpu.VMEM),
        scratch_shapes=[
            pltpu.SMEM(match.shape, jnp.int32),
            pltpu.SMEM(remap_offs.shape, jnp.int32),
            pltpu.SMEM(remap_count.shape, jnp.int32),
            pltpu.VMEM((rows, NBMAX, blk, blk), F32),
            pltpu.VMEM((2, levels * rows, blk), F32),
            pltpu.VMEM((2, levels, 2 * levels), F32),
            pltpu.VMEM((2, STEPS, levels), F32),
            pltpu.VMEM((2, 1, levels), F32),
            pltpu.VMEM((2, 2, HALF, blk), F32),
            pltpu.VMEM((2, 2, HALF, blk), F32),
            pltpu.VMEM((nz, HALF, GROUP, blk), F32),
            pltpu.VMEM((2, GROUP, blk), F32),
            pltpu.VMEM((2, blk), F32),
            pltpu.VMEM((nz, 2, blk), F32),
            pltpu.VMEM((nz * GROUP, blk), F32),
            pltpu.VMEM((nw, HALF, 2, blk), F32),
            pltpu.VMEM((nw, HALF, 2, blk), F32),
            pltpu.VMEM((2, HALF, 2, blk), F32),
            pltpu.VMEM((nw, GROUP, blk), F32),
            pltpu.VMEM((nw, GROUP, blk), F32),
            pltpu.VMEM((2, GROUP, blk), F32),
            pltpu.VMEM((GROUP, blk), F32),
            dma((8,)),
            dma((4,)),
            dma((4,)),
        ]
        + [dma] * 14,
        compiler_params=pltpu.CompilerParams(
            has_side_effects=True, collective_id=0, vmem_limit_bytes=32 << 20
        ),
    )(
        match,
        remap_offs,
        remap_count,
        adj_final.reshape(levels * rows, blk),
        flipped_vertical_steppers,
        profiles,
        skin_sensitivity_pair,
        conserving_transfer_factors,
    )
    return out.reshape(1, levels, cells)


def solution(mesh):
    return jax.shard_map(
        on_device,
        mesh=mesh,
        in_specs=(
            P("comp", "lev", "tile"),
            P("comp", "lev", None),
            P("comp", None, "lev"),
            P("comp", "lev"),
            P(),
            P("tile", None),
            P("tile"),
            P("tile", None, None, None),
        ),
        out_specs=P("comp", "lev", "tile"),
        check_vma=False,
    )
```

time: 1730 us -> 32.7 us (0.02)
  the two profiles are of different devices: /device:TPU:2 before, /device:TPU:1 now
where the time goes in v2:
time: 32.7 us; the launch traced here: 32.4 us
  Pallas kernels  29.2 us (89%)
  local copies, waits for them, and re-layouts  3.14 us (10%)
    pallas_call x1, Pallas kernels, on_device(): pl.pallas_call(functools.partial(kernel, nz, nw), out_shape=jax.ShapeDtyp...  29.2 us
    unnamed x15, local copies, waits for them, and re-layouts  3.14 us

profile of v2, /device:TPU:1, one launch (start us, length us, event | category | flops | bytes accessed | tf_op | source)
XLA Modules:
  0.0 32.4 jit_solution(3722298518746269799)
XLA Ops:
  0.0 0.0 copy-start.1
  0.0 0.7 %copy.13.profile_hbm = f32[1,6,36]{2,1,0:T(8,128)S(1)} copy(f32[1,6,36]{2,0,1:T(1,128)} %param.10) | data formatting | bytes 1728 | tf_op args[2]
  0.7 0.0 copy-start.2
  0.7 0.0 copy-start.3
  0.7 0.0 copy-start.4
  0.7 0.0 copy-start.5
  0.7 0.8 %copy.12.operator_hbm = f32[1,36,72]{2,1,0:T(8,128)S(1)} copy(f32[1,36,72]{2,0,1:T(1,128)} %param.9) | data formatting | bytes 20736 | tf_op args[1]
  1.5 0.0 copy-done.1
  1.5 0.0 copy-done.2
  1.5 0.0 copy-done.3
  1.5 0.0 copy-done.4
  1.5 0.0 copy-done.5
  1.5 0.0 copy-start
  1.5 1.0 %copy-done = f32[2,4,128,128]{3,2,1,0:T(8,128)S(1)} copy-done((f32[2,4,128,128]{3,2,1,0:T(8,128)S(1)}, f32[2,4,128,128]{3,2,1,0:T(8,128)}, u32[]{:S(2)}) %copy-start) | copy-done | bytes 524312
  2.6 29.2 %shard_map.82 = f32[72,128]{1,0:T(8,128)S(1)} custom-call(s32[128]{0:T(128)S(1)} %copy-done.3, s32[2,4]{1,0:T(2,128)S(1)} %copy-done.2, s32[2]{0:T(128)S(1)} %copy-done.4, f32[72,128]{1,0:T(8,128)S(1)} %bitcast.3, f32[1,36,72]{2,1,0:T(8,128)S(1)} %copy.12.operator_hbm, f32[1,6,36]{2,1,0:T(8,128)S(1)} %copy.13.profile_hbm, f32[1,36]{1,0:T(1,128)S(1)} %copy-done.5, ...), custom_call_target="tpu_custom_call" | custom-call | tf_op jit(solution)/shard_map/pallas_call | solution.py:374
  31.8 0.6 %copy.16 = f32[1,36,256]{2,0,1:T(1,128)} copy(f32[1,36,256]{2,0,1:T(1,128)S(1)} %bitcast.2) | data formatting | bytes 73728
Async XLA Ops:
  0.0 1.5 %copy-start.1 = (f32[1,36,256]{2,0,1:T(1,128)S(1)}, f32[1,36,256]{2,0,1:T(1,128)}, u32[]{:S(2)}) copy-start(f32[1,36,256]{2,0,1:T(1,128)} %param.8) | copy-start | bytes 110596
  0.7 0.8 %copy-start.2 = (s32[2,4]{1,0:T(2,128)S(1)}, s32[2,4]{1,0:T(2,128)}, u32[]{:S(2)}) copy-start(s32[2,4]{1,0:T(2,128)} %offs_hbm.1) | copy-start | bytes 100
  0.7 0.8 %copy-start.3 = (s32[128]{0:T(128)S(1)}, s32[128]{0:T(128)}, u32[]{:S(2)}) copy-start(s32[128]{0:T(128)} %match_hbm.1) | copy-start | bytes 1540
  0.7 0.8 %copy-start.4 = (s32[2]{0:T(128)S(1)}, s32[2]{0:T(128)}, u32[]{:S(2)}) copy-start(s32[2]{0:T(128)} %count_hbm.1) | copy-start | bytes 28
  0.7 0.8 %copy-start.5 = (f32[1,36]{1,0:T(1,128)S(1)}, f32[1,36]{1,0:T(1,128)}, u32[]{:S(2)}) copy-start(f32[1,36]{1,0:T(1,128)} %skin_hbm.1) | copy-start | bytes 436
  1.5 1.0 %copy-start = (f32[2,4,128,128]{3,2,1,0:T(8,128)S(1)}, f32[2,4,128,128]{3,2,1,0:T(8,128)}, u32[]{:S(2)}) copy-start(f32[2,4,128,128]{3,2,1,0:T(8,128)} %factors_hbm.1) | copy-start | bytes 1572868

commit v3 on v2

--- a/solution.py
+++ b/solution.py
@@ -90,8 +90,15 @@
     levels = operators.shape[1]
     blk = factors.shape[2]
     rows = factors.shape[0]
-    column = [((z + k) % nz) * nw + w for k in range(nz)]
-    row = [z * nw + (w + k) % nw for k in range(nw)]
+    ny = nw // 2
+    far = sorted(range(nz), key=lambda k: -min(k, nz - k))
+    column = [((z + k) % nz) * nw + w for k in far]
+    far = sorted(
+        ((i, k) for i in range(2) for k in range(ny)),
+        key=lambda ik: -(2 * ik[0] + min(ik[1], ny - ik[1])),
+    )
+    steps = [((w // ny + i) % 2) * ny + (w % ny + k) % ny for i, k in far]
+    row = [z * nw + q for q in steps]
     atmos, ocean = comp == 0, comp == 1
 
     def remote(src, dst, send, recv, to_comp, to_tile, to_lev):
@@ -115,8 +122,8 @@
         for i, (src, dst) in enumerate(
             (
                 (adj_hbm, state.at[lev]),
-                (profile_hbm.at[0], profiles.at[lev]),
-                (operator_hbm.at[0], operators.at[lev]),
+                (profile_hbm, profiles.at[lev]),
+                (operator_hbm, operators.at[lev]),
                 (skin_hbm, skins.at[lev]),
                 (factors_hbm, factors),
                 (offs_hbm, offs_ref),
@@ -147,14 +154,14 @@
     def _():
         for to in column:
             greet(0, to, lev)
-        for to in column[1:] + row[1:]:
+        for to in column[:-1] + row[:-1]:
             greet(1, to, lev)
         pl.semaphore_wait(barrier, nz + 2 * nw - 1)
 
     pairs = (
         (adj_hbm, state),
-        (operator_hbm.at[0], operators),
-        (profile_hbm.at[0], profiles),
+        (operator_hbm, operators),
+        (profile_hbm, profiles),
         (skin_hbm, skins),
     )
 
@@ -166,8 +173,8 @@
             load.wait()
         for i in (1, 2, 3):
             settle(pairs[i][1].at[0], pair_recv.at[i])
-        whole = jnp.concatenate([operators[0], operators[1]], axis=0)
-        profile_rows = jnp.concatenate([profiles[0], profiles[1]], axis=1)
+        whole = jnp.concatenate([operators[0, :, 0], operators[1, :, 0]], axis=0)
+        profile_rows = jnp.concatenate([profiles[0, :, 0], profiles[1, :, 0]], axis=1)
 
         power = jnp.concatenate([skins[0], skins[1]], axis=1)
         total = power
@@ -185,7 +192,7 @@
         for to in column:
             remote(sigma_own, sigma_in.at[z], sigma_send, sigma_recv, 1, to, lev)
 
-        power = operators[lev]
+        power = operators[lev, :, 0]
         shares = []
         for s in range(STEPS):
             if s > 0:
@@ -222,7 +229,7 @@
             load.wait()
         own = halves(state.at[lev])
         for h in range(2):
-            partial = dot(profiles[lev], own[h])
+            partial = dot(profiles[lev, :, 0], own[h])
             for half in range(2):
                 flux_part[half, h] = partial[half * HALF : (half + 1) * HALF]
         remote(
@@ -253,7 +260,7 @@
             contrib_in[z, s, :REACH] = jnp.concatenate(
                 [totals[b][s : s + 1] for b in range(REACH)], axis=0
             )
-        for to in column[1:]:
+        for to in column[:-1]:
             remote(
                 contrib_in.at[z, :, pl.ds(0, REACH)],
                 contrib_in.at[z, :, pl.ds(0, REACH)],
@@ -293,7 +300,7 @@
         settle(state.at[0], pair_recv.at[0])
         first, second = halves(state.at[0]), halves(state.at[1])
         bases = [
-            dot(operators[lev], jnp.concatenate([first[h], second[h]], axis=0)) for h in range(2)
+            dot(operators[lev, :, 0], jnp.concatenate([first[h], second[h]], axis=0)) for h in range(2)
         ]
         skin_column = jnp.broadcast_to(column_of(skins[lev]), (levels, blk))
 
@@ -305,7 +312,7 @@
                 flux_out[q, s] = picked[2 * q : 2 * q + 2]
         for k in range(nw):
             remote(
-                flux_out.at[(w + k) % nw], flux_in.at[w], flux_send, flux_recv, 0, row[k], lev
+                flux_out.at[steps[k]], flux_in.at[w], flux_send, flux_recv, 0, row[k], lev
             )
         settle(weight_in.at[0], weight_recv)
         total = jnp.zeros((size, blk), F32)
@@ -319,9 +326,9 @@
         for i in range(nz):
             mixed[i * GROUP + REACH : (i + 1) * GROUP] = sigma_in[i]
         heat_out[...] = dot(to_ocean, mixed[...]).reshape(nw, GROUP, blk)
-        for k in range(1, nw):
+        for k in range(nw - 1):
             remote(
-                heat_out.at[(w + k) % nw], heat_in.at[w], heat_send, heat_recv, 1, row[k], lev
+                heat_out.at[steps[k]], heat_in.at[w], heat_send, heat_recv, 1, row[k], lev
             )
         heat_in[w] = heat_out[w]
         settle(heat_in.at[: nw - 1], heat_recv)
@@ -371,6 +378,16 @@
     rows, _, blk, _ = conserving_transfer_factors.shape
     hbm = pl.BlockSpec(memory_space=pltpu.HBM)
     dma = pltpu.SemaphoreType.DMA
+    arrays = (
+        match,
+        remap_offs,
+        remap_count,
+        adj_final.reshape(levels * rows, blk),
+        flipped_vertical_steppers.reshape(levels, 1, 2 * levels),
+        profiles.reshape(STEPS, 1, levels),
+        skin_sensitivity_pair,
+        conserving_transfer_factors,
+    )
     out = pl.pallas_call(
         functools.partial(kernel, nz, nw),
         out_shape=jax.ShapeDtypeStruct((levels * rows, blk), F32),
@@ -382,8 +399,8 @@
             pltpu.SMEM(remap_count.shape, jnp.int32),
             pltpu.VMEM((rows, NBMAX, blk, blk), F32),
             pltpu.VMEM((2, levels * rows, blk), F32),
-            pltpu.VMEM((2, levels, 2 * levels), F32),
-            pltpu.VMEM((2, STEPS, levels), F32),
+            pltpu.VMEM((2, levels, 1, 2 * levels), F32),
+            pltpu.VMEM((2, STEPS, 1, levels), F32),
             pltpu.VMEM((2, 1, levels), F32),
             pltpu.VMEM((2, 2, HALF, blk), F32),
             pltpu.VMEM((2, 2, HALF, blk), F32),
@@ -408,14 +425,7 @@
             has_side_effects=True, collective_id=0, vmem_limit_bytes=32 << 20
         ),
     )(
-        match,
-        remap_offs,
-        remap_count,
-        adj_final.reshape(levels * rows, blk),
-        flipped_vertical_steppers,
-        profiles,
-        skin_sensitivity_pair,
-        conserving_transfer_factors,
+        *(pltpu.with_memory_space_constraint(array, pltpu.HBM) for array in arrays)
     )
     return out.reshape(1, levels, cells)
 

time: 32.7 us -> 29.6 us (0.905)
  local copies, waits for them, and re-layouts: 3.14 us -> 0.62 us
    unnamed x15 -> x1, local copies, waits for them, and re-layouts: 3.14 us -> 0.62 us
    pallas_call x1, Pallas kernels: 29.2 us -> 28.9 us  [on_device(): pl.pallas_call(functools.partial(kernel, nz, nw), out_shape=jax.ShapeDtyp...]
where the time goes in v3:
time: 29.6 us; the launch traced here: 29.5 us
  Pallas kernels  28.9 us (98%)
  local copies, waits for them, and re-layouts  0.62 us (2%)
    pallas_call x1, Pallas kernels, on_device(): pl.pallas_call(functools.partial(kernel, nz, nw), out_shape=jax.ShapeDtyp...  28.9 us
    unnamed x1, local copies, waits for them, and re-layouts  0.62 us

profile of v3, /device:TPU:1, one launch (start us, length us, event | category | flops | bytes accessed | tf_op | source)
XLA Modules:
  0.0 29.5 jit_solution(8052753561000360254)
XLA Ops:
  0.0 28.9 %shard_map.82 = f32[72,128]{1,0:T(8,128)S(1)} custom-call(s32[128]{0:T(128)} %match_hbm.1, s32[2,4]{1,0:T(2,128)} %offs_hbm.1, s32[2]{0:T(128)} %count_hbm.1, f32[72,128]{1,0:T(8,128)} %bitcast.5, f32[36,1,72]{2,1,0:T(1,128)} %bitcast.6, f32[6,1,36]{2,1,0:T(1,128)} %bitcast.7, f32[1,36]{1,0:T(1,128)} %skin_hbm.1, f32[2,4,128,128]{3,2,1,0:T(8,128)} %factors_hbm.1), custom_call_target="tpu_custom_call" | custom-call | tf_op jit(solution)/shard_map/pallas_call | solution.py:391
  28.9 0.6 %copy.12 = f32[1,36,256]{2,0,1:T(1,128)} copy(f32[1,36,256]{2,0,1:T(1,128)S(1)} %bitcast.4) | data formatting | bytes 73728

commit v4 on v3

--- a/solution.py
+++ b/solution.py
@@ -19,6 +19,17 @@
 
 def dot(a, b):
     return jnp.dot(a, b, precision=HIGHEST, preferred_element_type=F32)
+
+
+def pick(hits, values):
+    hits = hits.astype(jnp.bfloat16)
+    total = None
+    for _ in range(3):
+        part = values.astype(jnp.bfloat16)
+        values = values - part.astype(F32)
+        term = jnp.dot(hits, part, preferred_element_type=F32)
+        total = term if total is None else total + term
+    return total
 
 
 def column_of(row):
@@ -95,7 +106,7 @@
     column = [((z + k) % nz) * nw + w for k in far]
     far = sorted(
         ((i, k) for i in range(2) for k in range(ny)),
-        key=lambda ik: -(2 * ik[0] + min(ik[1], ny - ik[1])),
+        key=lambda ik: (-min(ik[1], ny - ik[1]), -ik[0]),
     )
     steps = [((w // ny + i) % 2) * ny + (w % ny + k) % ny for i, k in far]
     row = [z * nw + q for q in steps]
@@ -132,9 +143,6 @@
             )
         )
     ]
-    for load in loads:
-        load.start()
-
     barrier = pltpu.get_barrier_semaphore()
 
     def greet(to_comp, to_tile, to_lev):
@@ -148,6 +156,10 @@
     def _():
         for to in row:
             greet(1, to, lev)
+        for load in loads:
+            load.start()
+        for load in loads[:4]:
+            load.wait()
         pl.semaphore_wait(barrier, 1 + nz)
 
     @pl.when(ocean)
@@ -156,32 +168,52 @@
             greet(0, to, lev)
         for to in column[:-1] + row[:-1]:
             greet(1, to, lev)
+        for load in loads:
+            load.start()
+        contrib_in[:, :, REACH:] = jnp.zeros((nz, HALF, GROUP - REACH, blk), F32)
+        for load in loads[:2] + loads[4:]:
+            load.wait()
+        own = halves(state.at[lev])
+        totals = [jnp.zeros((STEPS, blk), F32) for _ in range(REACH)]
+        for r in range(rows):
+            flux = dot(profiles[lev, :, 0], own[r])
+            flux = jnp.concatenate([flux, jnp.zeros((GROUP - STEPS, blk), F32)], axis=0).T
+            columns = [jnp.broadcast_to(flux[:, s : s + 1], (blk, blk)) for s in range(STEPS)]
+            for e in range(NBMAX):
+                block = factors[r, e]
+                part = jnp.concatenate(
+                    [jnp.sum(block * columns[s], axis=0, keepdims=True) for s in range(STEPS)],
+                    axis=0,
+                )
+                offset = jnp.where(e < count_ref[r], offs_ref[r, e], -1)
+                for b in range(REACH):
+                    totals[b] = totals[b] + part * (offset == b).astype(F32)
+        for s in range(STEPS):
+            flux_part[s // HALF, s % HALF] = jnp.concatenate(
+                [totals[b][s : s + 1] for b in range(REACH)], axis=0
+            )
         pl.semaphore_wait(barrier, nz + 2 * nw - 1)
 
-    pairs = (
-        (adj_hbm, state),
-        (operator_hbm, operators),
-        (profile_hbm, profiles),
-        (skin_hbm, skins),
-    )
+    pairs = (state, operators, profiles, skins)
 
     @pl.when(atmos)
     def _():
-        for i, (src, dst) in ((1, pairs[1]), (3, pairs[3]), (2, pairs[2]), (0, pairs[0])):
-            remote(src, dst.at[lev], pair_send.at[i], pair_recv.at[i], 0, tile, 1 - lev)
-        for load in loads[:4]:
-            load.wait()
+        for i in (1, 3, 2, 0):
+            ref = pairs[i].at[lev]
+            remote(ref, ref, pair_send.at[i], pair_recv.at[i], 0, tile, 1 - lev)
         for i in (1, 2, 3):
-            settle(pairs[i][1].at[0], pair_recv.at[i])
+            settle(pairs[i].at[0], pair_recv.at[i])
         whole = jnp.concatenate([operators[0, :, 0], operators[1, :, 0]], axis=0)
         profile_rows = jnp.concatenate([profiles[0, :, 0], profiles[1, :, 0]], axis=1)
 
-        power = jnp.concatenate([skins[0], skins[1]], axis=1)
-        total = power
+        first = jnp.concatenate([skins[0], skins[1]], axis=1)
+        first = jnp.concatenate([first, dot(first, whole)], axis=0)
+        square = dot(whole, whole)
+        second = dot(first, square)
+        chain = (first, second, dot(second, square))
+        total = jnp.zeros((1, 2 * levels), F32)
         for s in range(STEPS):
-            if s > 0:
-                power = dot(power, whole)
-                total = total + power
+            total = total + chain[s // 2][s % 2 : s % 2 + 1]
             weight = jnp.sum(total * profile_rows[s : s + 1], axis=1, keepdims=True)
             weight_in[1, s : s + 1] = jnp.broadcast_to(weight, (1, blk))
         remote(weight_in.at[1], weight_in.at[0], weight_send, weight_recv, 1, tile, lev)
@@ -216,7 +248,7 @@
             out_ref[pl.ds(h, levels, stride=2), :] = total
 
         for i in range(4):
-            settle(pairs[i][1].at[0], pair_send.at[i])
+            settle(pairs[i].at[0], pair_send.at[i])
         settle(weight_in.at[0], weight_send)
         settle(sigma_in, sigma_send)
         settle(flux_sum.at[0], last_send)
@@ -225,41 +257,11 @@
 
     @pl.when(ocean)
     def _():
-        for load in loads[:2]:
-            load.wait()
-        own = halves(state.at[lev])
-        for h in range(2):
-            partial = dot(profiles[lev, :, 0], own[h])
-            for half in range(2):
-                flux_part[half, h] = partial[half * HALF : (half + 1) * HALF]
         remote(
-            flux_part.at[1 - lev], flux_half.at[lev], part_send, part_recv, 1, tile, 1 - lev
+            flux_part.at[1 - lev], flux_half, part_send, part_recv, 1, tile, 1 - lev
         )
-        remote(adj_hbm, state.at[lev], pair_send.at[0], pair_recv.at[0], 1, tile, 1 - lev)
-        flux_half[lev] = flux_part[lev]
-        contrib_in[:, :, REACH:] = jnp.zeros((nz, HALF, GROUP - REACH, blk), F32)
-        for load in loads[4:]:
-            load.wait()
-        settle(flux_half.at[0], part_recv)
-
-        totals = [jnp.zeros((HALF, blk), F32) for _ in range(REACH)]
-        for r in range(rows):
-            flux = flux_half[0, r] + flux_half[1, r]
-            flux = jnp.concatenate([flux, jnp.zeros((GROUP - HALF, blk), F32)], axis=0).T
-            columns = [jnp.broadcast_to(flux[:, s : s + 1], (blk, blk)) for s in range(HALF)]
-            for e in range(NBMAX):
-                block = factors[r, e]
-                part = jnp.concatenate(
-                    [jnp.sum(block * columns[s], axis=0, keepdims=True) for s in range(HALF)],
-                    axis=0,
-                )
-                offset = jnp.where(e < count_ref[r], offs_ref[r, e], -1)
-                for b in range(REACH):
-                    totals[b] = totals[b] + part * (offset == b).astype(F32)
-        for s in range(HALF):
-            contrib_in[z, s, :REACH] = jnp.concatenate(
-                [totals[b][s : s + 1] for b in range(REACH)], axis=0
-            )
+        settle(flux_half, part_recv)
+        contrib_in[z, :, :REACH] = flux_part[lev] + flux_half[...]
         for to in column[:-1]:
             remote(
                 contrib_in.at[z, :, pl.ds(0, REACH)],
@@ -270,6 +272,8 @@
                 to,
                 lev,
             )
+
+        remote(state.at[lev], state.at[lev], pair_send.at[0], pair_recv.at[0], 1, tile, 1 - lev)
 
         size = nz * GROUP
         lane = lax.broadcasted_iota(jnp.int32, (GROUP, size), 1)
@@ -307,7 +311,7 @@
         settle(contrib_in.at[: nz - 1, :, pl.ds(0, REACH)], contrib_recv)
         column_data = [contrib_in[:, s].reshape(size, blk) for s in range(HALF)]
         for s in range(HALF):
-            picked = dot(to_atmos, column_data[s])
+            picked = pick(to_atmos, column_data[s])
             for q in range(nw):
                 flux_out[q, s] = picked[2 * q : 2 * q + 2]
         for k in range(nw):
@@ -325,7 +329,9 @@
         settle(sigma_in, sigma_recv)
         for i in range(nz):
             mixed[i * GROUP + REACH : (i + 1) * GROUP] = sigma_in[i]
-        heat_out[...] = dot(to_ocean, mixed[...]).reshape(nw, GROUP, blk)
+        warm = pick(to_ocean, mixed[...])
+        for q in range(nw):
+            heat_out[q] = warm[q * GROUP : q * GROUP + REACH]
         for k in range(nw - 1):
             remote(
                 heat_out.at[steps[k]], heat_in.at[w], heat_send, heat_recv, 1, row[k], lev
@@ -402,8 +408,8 @@
             pltpu.VMEM((2, levels, 1, 2 * levels), F32),
             pltpu.VMEM((2, STEPS, 1, levels), F32),
             pltpu.VMEM((2, 1, levels), F32),
-            pltpu.VMEM((2, 2, HALF, blk), F32),
-            pltpu.VMEM((2, 2, HALF, blk), F32),
+            pltpu.VMEM((2, HALF, REACH, blk), F32),
+            pltpu.VMEM((HALF, REACH, blk), F32),
             pltpu.VMEM((nz, HALF, GROUP, blk), F32),
             pltpu.VMEM((2, GROUP, blk), F32),
             pltpu.VMEM((2, blk), F32),
@@ -412,10 +418,10 @@
             pltpu.VMEM((nw, HALF, 2, blk), F32),
             pltpu.VMEM((nw, HALF, 2, blk), F32),
             pltpu.VMEM((2, HALF, 2, blk), F32),
-            pltpu.VMEM((nw, GROUP, blk), F32),
-            pltpu.VMEM((nw, GROUP, blk), F32),
-            pltpu.VMEM((2, GROUP, blk), F32),
-            pltpu.VMEM((GROUP, blk), F32),
+            pltpu.VMEM((nw, REACH, blk), F32),
+            pltpu.VMEM((nw, REACH, blk), F32),
+            pltpu.VMEM((2, REACH, blk), F32),
+            pltpu.VMEM((REACH, blk), F32),
             dma((8,)),
             dma((4,)),
             dma((4,)),

time: 29.6 us -> 29.1 us (0.983)
  Pallas kernels: 28.9 us -> 28.4 us
    pallas_call x1, Pallas kernels: 28.9 us -> 28.4 us  [on_device(): pl.pallas_call(functools.partial(kernel, nz, nw), out_shape=jax.ShapeDtyp...]
where the time goes in v4:
time: 29.1 us; the launch traced here: 29 us
  Pallas kernels  28.4 us (98%)
  local copies, waits for them, and re-layouts  0.62 us (2%)
    pallas_call x1, Pallas kernels, on_device(): pl.pallas_call(functools.partial(kernel, nz, nw), out_shape=jax.ShapeDtyp...  28.4 us
    unnamed x1, local copies, waits for them, and re-layouts  0.62 us

profile of v4, /device:TPU:1, one launch (start us, length us, event | category | flops | bytes accessed | tf_op | source)
XLA Modules:
  0.0 29.0 jit_solution(2196253455535005519)
XLA Ops:
  0.0 28.4 %shard_map.82 = f32[72,128]{1,0:T(8,128)S(1)} custom-call(s32[128]{0:T(128)} %match_hbm.1, s32[2,4]{1,0:T(2,128)} %offs_hbm.1, s32[2]{0:T(128)} %count_hbm.1, f32[72,128]{1,0:T(8,128)} %bitcast.5, f32[36,1,72]{2,1,0:T(1,128)} %bitcast.6, f32[6,1,36]{2,1,0:T(1,128)} %bitcast.7, f32[1,36]{1,0:T(1,128)} %skin_hbm.1, f32[2,4,128,128]{3,2,1,0:T(8,128)} %factors_hbm.1), custom_call_target="tpu_custom_call" | custom-call | tf_op jit(solution)/shard_map/pallas_call | solution.py:397
  28.4 0.6 %copy.12 = f32[1,36,256]{2,0,1:T(1,128)} copy(f32[1,36,256]{2,0,1:T(1,128)S(1)} %bitcast.4) | data formatting | bytes 73728

commit v5 on v4

--- a/solution.py
+++ b/solution.py
@@ -164,10 +164,10 @@
 
     @pl.when(ocean)
     def _():
+        for to in row[:-1] + column[:-1]:
+            greet(1, to, lev)
         for to in column:
             greet(0, to, lev)
-        for to in column[:-1] + row[:-1]:
-            greet(1, to, lev)
         for load in loads:
             load.start()
         contrib_in[:, :, REACH:] = jnp.zeros((nz, HALF, GROUP - REACH, blk), F32)
@@ -198,7 +198,7 @@
 
     @pl.when(atmos)
     def _():
-        for i in (1, 3, 2, 0):
+        for i in (1, 3, 2):
             ref = pairs[i].at[lev]
             remote(ref, ref, pair_send.at[i], pair_recv.at[i], 0, tile, 1 - lev)
         for i in (1, 2, 3):
@@ -223,6 +223,8 @@
             sigma_own[h : h + 1] = dot(mine, own[h])
         for to in column:
             remote(sigma_own, sigma_in.at[z], sigma_send, sigma_recv, 1, to, lev)
+        ref = state.at[lev]
+        remote(ref, ref, pair_send.at[0], pair_recv.at[0], 0, tile, 1 - lev)
 
         power = operators[lev, :, 0]
         shares = []
@@ -299,15 +301,6 @@
             picks.append(hit.astype(F32))
         to_ocean = jnp.concatenate(picks, axis=0)
 
-        for load in loads[2:4]:
-            load.wait()
-        settle(state.at[0], pair_recv.at[0])
-        first, second = halves(state.at[0]), halves(state.at[1])
-        bases = [
-            dot(operators[lev, :, 0], jnp.concatenate([first[h], second[h]], axis=0)) for h in range(2)
-        ]
-        skin_column = jnp.broadcast_to(column_of(skins[lev]), (levels, blk))
-
         settle(contrib_in.at[: nz - 1, :, pl.ds(0, REACH)], contrib_recv)
         column_data = [contrib_in[:, s].reshape(size, blk) for s in range(HALF)]
         for s in range(HALF):
@@ -336,6 +329,15 @@
             remote(
                 heat_out.at[steps[k]], heat_in.at[w], heat_send, heat_recv, 1, row[k], lev
             )
+        for load in loads[2:4]:
+            load.wait()
+        settle(state.at[0], pair_recv.at[0])
+        first, second = halves(state.at[0]), halves(state.at[1])
+        bases = [
+            dot(operators[lev, :, 0], jnp.concatenate([first[h], second[h]], axis=0)) for h in range(2)
+        ]
+        skin_column = jnp.broadcast_to(column_of(skins[lev]), (levels, blk))
+
         heat_in[w] = heat_out[w]
         settle(heat_in.at[: nw - 1], heat_recv)
         total = heat_in[0]

time: 29.1 us -> 29.2 us (level)
  no operation moved by 1% of the time
where the time goes in v5:
time: 29.2 us; the launch traced here: 29 us
  Pallas kernels  28.4 us (97%)
  local copies, waits for them, and re-layouts  0.62 us (2%)
    pallas_call x1, Pallas kernels, on_device(): pl.pallas_call(functools.partial(kernel, nz, nw), out_shape=jax.ShapeDtyp...  28.4 us
    unnamed x1, local copies, waits for them, and re-layouts  0.62 us

profile of v5, /device:TPU:1, one launch (start us, length us, event | category | flops | bytes accessed | tf_op | source)
XLA Modules:
  0.0 29.0 jit_solution(6886164944210619325)
XLA Ops:
  0.0 28.4 %shard_map.82 = f32[72,128]{1,0:T(8,128)S(1)} custom-call(s32[128]{0:T(128)} %match_hbm.1, s32[2,4]{1,0:T(2,128)} %offs_hbm.1, s32[2]{0:T(128)} %count_hbm.1, f32[72,128]{1,0:T(8,128)} %bitcast.5, f32[36,1,72]{2,1,0:T(1,128)} %bitcast.6, f32[6,1,36]{2,1,0:T(1,128)} %bitcast.7, f32[1,36]{1,0:T(1,128)} %skin_hbm.1, f32[2,4,128,128]{3,2,1,0:T(8,128)} %factors_hbm.1), custom_call_target="tpu_custom_call" | custom-call | tf_op jit(solution)/shard_map/pallas_call | solution.py:399
  28.4 0.6 %copy.12 = f32[1,36,256]{2,0,1:T(1,128)} copy(f32[1,36,256]{2,0,1:T(1,128)S(1)} %bitcast.4) | data formatting | bytes 73728

commit v6 on v5

--- a/solution.py
+++ b/solution.py
@@ -226,15 +226,23 @@
         ref = state.at[lev]
         remote(ref, ref, pair_send.at[0], pair_recv.at[0], 0, tile, 1 - lev)
 
-        power = operators[lev, :, 0]
+        mine = operators[lev, :, 0]
+        flux_columns = jnp.concatenate(
+            [profile_rows, jnp.zeros((GROUP - STEPS, 2 * levels), F32)], axis=0
+        ).T
         shares = []
         for s in range(STEPS):
             if s > 0:
-                power = dot(power, whole)
-            shares.append(jnp.sum(power * profile_rows[s : s + 1], axis=1, keepdims=True))
+                flux_columns = dot(whole, flux_columns)
+            shares.append(dot(mine, flux_columns)[:, s : s + 1])
         settle(state.at[0], pair_recv.at[0])
         first, second = halves(state.at[0]), halves(state.at[1])
-        bases = [dot(power, jnp.concatenate([first[h], second[h]], axis=0)) for h in range(2)]
+        bases = []
+        for h in range(2):
+            moved = jnp.concatenate([first[h], second[h]], axis=0)
+            for _ in range(STEPS - 1):
+                moved = dot(whole, moved)
+            bases.append(dot(mine, moved))
 
         settle(flux_in, flux_recv)
         total = flux_in[0]

time: 29.2 us -> 29.1 us (level)
  no operation moved by 1% of the time
where the time goes in v6:
time: 29.1 us; the launch traced here: 29 us
  Pallas kernels  28.4 us (98%)
  local copies, waits for them, and re-layouts  0.62 us (2%)
    pallas_call x1, Pallas kernels, on_device(): pl.pallas_call(functools.partial(kernel, nz, nw), out_shape=jax.ShapeDtyp...  28.4 us
    unnamed x1, local copies, waits for them, and re-layouts  0.62 us

profile of v6, /device:TPU:1, one launch (start us, length us, event | category | flops | bytes accessed | tf_op | source)
XLA Modules:
  0.0 29.0 jit_solution(3062884872423838924)
XLA Ops:
  0.0 28.4 %shard_map.82 = f32[72,128]{1,0:T(8,128)S(1)} custom-call(s32[128]{0:T(128)} %match_hbm.1, s32[2,4]{1,0:T(2,128)} %offs_hbm.1, s32[2]{0:T(128)} %count_hbm.1, f32[72,128]{1,0:T(8,128)} %bitcast.5, f32[36,1,72]{2,1,0:T(1,128)} %bitcast.6, f32[6,1,36]{2,1,0:T(1,128)} %bitcast.7, f32[1,36]{1,0:T(1,128)} %skin_hbm.1, f32[2,4,128,128]{3,2,1,0:T(8,128)} %factors_hbm.1), custom_call_target="tpu_custom_call" | custom-call | tf_op jit(solution)/shard_map/pallas_call | solution.py:407
  28.4 0.6 %copy.12 = f32[1,36,256]{2,0,1:T(1,128)} copy(f32[1,36,256]{2,0,1:T(1,128)S(1)} %bitcast.4) | data formatting | bytes 73728
